TPU v7x, 32 devices: a whole 2x2x4 slice. The times are simulated.
32 devices in a mesh: gx: 8 (over y, x, core), sp: 4 (over z).
Axes of the slice: x: 2, y: 2, z: 4, core: 2. Of those that a mesh axis runs over, the one named last changes fastest.
Arguments:
- previous_head: float32 [8, 64, 512], P(None, 'gx', 'sp'), may hold values from -6 to 6
- recharge: float32 [8, 64, 512], P(None, 'gx', 'sp'), may hold values from -6 to 6
- soil_zone: int32 [8, 64, 512], P(None, 'gx', 'sp'), may hold values from 0 to 7
- soil_cond: float32 [8], replicated, may hold values from 0.1 to 1
- soil_store: float32 [8], replicated, may hold values from 0.05 to 0.5
- species: float32 [12, 8, 64, 512], P('sp', None, 'gx'), may hold values from -6 to 6
- mineral_zone: int32 [8, 64, 512], P(None, 'gx', 'sp'), may hold values from 0 to 5
- rate_table: float32 [6, 8], replicated, may hold values from 0.3 to 3
- stoich: float32 [12, 8], replicated, may hold values from -3 to 3
- log_equil: float32 [8], replicated, may hold values from -1 to 1
Outputs:
- head_field: float32 [8, 64, 512], P(None, 'gx', 'sp')
- species_out: float32 [12, 8, 64, 512], P('sp', None, 'gx')
Inputs may be any that keep to these rules, and one draw needn't show every extreme that they name: `soil_zone`: a soil class of 8. `mineral_zone`: a mineral zone class of 6.
All inputs are finite; a program needn't handle non-finite values.
Results may differ from a plain program's by a relative error of at most 0.0003.
Values sent between devices are 32-bit elements; how exact they have to be, the bound alone decides.
No kernel may reach another device: no remote copies, remote signals or barrier semaphores. Data moves between devices by JAX's collectives and lax.ppermute only.
A program may use at most 64 MiB of HBM per device.

v0:
```python
import jax
import jax.numpy as jnp
from jax import lax
from jax.sharding import PartitionSpec as P

ITERS = 6
NEWTON = 2
time_step = 0.05
dispersion = 0.5
reaction_span = 0.5
newton_damping = 0.5


def padded_2(cells, sides, width):
    for axis, dim in sides:
        count = lax.axis_size(axis)
        ends = count - 1
        head = lax.slice_in_dim(cells, 0, width, axis=dim)
        tail = lax.slice_in_dim(cells, cells.shape[dim] - width, cells.shape[dim], axis=dim)
        cells = jnp.concatenate(
            [
                lax.ppermute(tail, axis, [(i, (i + 1) % count) for i in range(ends)]),
                cells,
                lax.ppermute(head, axis, [((i + 1) % count, i) for i in range(ends)]),
            ],
            axis=dim,
        )
    return cells


def harmonic(center, other):
    return 2.0 * center * other / (center + other)


def six_sides(padded):
    return [
        padded[..., 2:, 1:-1, 1:-1],
        padded[..., :-2, 1:-1, 1:-1],
        padded[..., 1:-1, 2:, 1:-1],
        padded[..., 1:-1, :-2, 1:-1],
        padded[..., 1:-1, 1:-1, 2:],
        padded[..., 1:-1, 1:-1, :-2],
    ]


def lookup(labels, entries):
    levels = jnp.arange(entries.shape[0], dtype=jnp.int32).reshape((-1,) + (1,) * labels.ndim)
    return jnp.sum(jnp.where(labels[None] == levels, entries.reshape(levels.shape), 0.0), axis=0)


def lookup_rows(labels, entries):
    levels = jnp.arange(entries.shape[0], dtype=jnp.int32)[:, None, None]
    return jnp.sum(jnp.where(labels[None, None, :] == levels, entries[:, :, None], 0.0), axis=0)


def transport(concentration, conc_padded, head_padded, cond_padded):
    head_center = head_padded[1:-1, 1:-1, 1:-1]
    conduct = cond_padded[1:-1, 1:-1, 1:-1]
    change = jnp.zeros_like(concentration)
    for beside, head_beside, cond_beside in zip(
        six_sides(conc_padded), six_sides(head_padded), six_sides(cond_padded)
    ):
        face_cond = harmonic(conduct, cond_beside)
        velocity = face_cond * (head_center - head_beside)
        change = (
            change
            + jnp.maximum(velocity, 0.0) * concentration
            + jnp.minimum(velocity, 0.0) * beside
        )
        change = change + dispersion * face_cond * (concentration - beside)
    return concentration - time_step * change


def solve_system(jacobian, mismatch):
    dimension = mismatch.shape[0]
    factor = [[None] * dimension for i in range(dimension)]
    inverse = [None] * dimension
    for j in range(dimension):
        for i in range(j, dimension):
            running = jacobian[i * dimension + j] + (1.0 if i == j else 0.0)
            for k in range(j):
                running = running - factor[i][k] * factor[j][k]
            if i == j:
                diag_root = jnp.sqrt(running)
                factor[j][j] = diag_root
                inverse[j] = 1.0 / diag_root
            else:
                factor[i][j] = running * inverse[j]
    forward = []
    for i in range(dimension):
        running = mismatch[i]
        for k in range(i):
            running = running - factor[i][k] * forward[k]
        forward.append(running * inverse[i])
    answer = [None] * dimension
    for i in reversed(range(dimension)):
        running = forward[i]
        for k in range(i + 1, dimension):
            running = running - factor[k][i] * answer[k]
        answer[i] = running * inverse[i]
    return jnp.stack(answer, 0)


def reaction(concentration, labels, rate_table, stoich, log_equil):
    rate_cells = lookup_rows(labels, rate_table)
    pair_products = (stoich[:, None, :] * stoich[None, :, :]).reshape(-1, stoich.shape[1])
    iterate = concentration
    for newton_pass in range(NEWTON):
        affinity = (
            jnp.dot(
                stoich.T,
                iterate,
                precision=lax.Precision.HIGHEST,
                preferred_element_type=jnp.float32,
            )
            - log_equil[:, None]
        )
        tangent = jnp.tanh(affinity)
        mismatch = (
            iterate
            - concentration
            + reaction_span
            * jnp.dot(
                stoich,
                rate_cells * tangent,
                precision=lax.Precision.HIGHEST,
                preferred_element_type=jnp.float32,
            )
        )
        jacobian = reaction_span * jnp.dot(
            pair_products,
            rate_cells * (1.0 - tangent * tangent),
            precision=lax.Precision.HIGHEST,
            preferred_element_type=jnp.float32,
        )
        iterate = iterate - newton_damping * solve_system(jacobian, mismatch)
    return iterate


def pad_vertical(field):
    return jnp.pad(field, ((1, 1), (0, 0), (0, 0)))


def to_cells(block):
    return lax.all_to_all(block, "sp", split_axis=3, concat_axis=0, tiled=True)


def per_device(
    previous_head,
    recharge,
    soil_zone,
    soil_cond,
    soil_store,
    species,
    mineral_zone,
    rate_table,
    stoich,
    log_equil,
):
    conduct = lookup(soil_zone, soil_cond)
    storage = lookup(soil_zone, soil_store)
    cond_padded = pad_vertical(padded_2(conduct, (("gx", 1), ("sp", 2)), 1))
    faces = [harmonic(conduct, beside) for beside in six_sides(cond_padded)]

    def operate(field):
        padded = pad_vertical(padded_2(field, (("gx", 1), ("sp", 2)), 1))
        result = storage * field
        for face_cond, beside in zip(faces, six_sides(padded)):
            result = result + face_cond * (field - beside)
        return result

    source = storage * previous_head + recharge
    head_field = jnp.zeros_like(source)
    residual = source

    def inner_pair(first, second):
        return lax.psum((jnp.sum(first * first), jnp.sum(first * second)), ("gx", "sp"))

    image = operate(residual)
    norm_now, product = inner_pair(residual, image)
    alpha = norm_now / product
    direction = residual
    along = image
    for iteration in range(ITERS):
        head_field = head_field + alpha * direction
        residual = residual - alpha * along
        if iteration + 1 < ITERS:
            image = operate(residual)
            norm_next, product = inner_pair(residual, image)
            ratio = norm_next / norm_now
            alpha = norm_next / (product - ratio * norm_next / alpha)
            direction = residual + ratio * direction
            along = image + ratio * along
            norm_now = norm_next
    head_rows, cond_rows = (
        lax.all_gather(head_field, "sp", axis=2, tiled=True),
        lax.all_gather(conduct, "sp", axis=2, tiled=True),
    )
    stacked = jnp.concatenate([species, head_rows[None], cond_rows[None]], 0)
    padded = padded_2(stacked, (("gx", 2),), 1)
    padded = jnp.pad(padded, ((0, 0), (1, 1), (0, 0), (1, 1)))
    moved = transport(species, padded[:-2], padded[-2], padded[-1])
    cells = to_cells(moved)
    block_shape = cells.shape
    reacted = reaction(
        cells.reshape(block_shape[0], -1), mineral_zone.reshape(-1), rate_table, stoich, log_equil
    )
    reacted = reacted.reshape(block_shape)
    species_out = lax.all_to_all(reacted, "sp", split_axis=0, concat_axis=3, tiled=True)
    return (head_field, species_out)


def solution(mesh):
    in_specs = (
        P(None, "gx", "sp"),
        P(None, "gx", "sp"),
        P(None, "gx", "sp"),
        P(),
        P(),
        P("sp", None, "gx", None),
        P(None, "gx", "sp"),
        P(),
        P(),
        P(),
    )
    out_specs = (P(None, "gx", "sp"), P("sp", None, "gx", None))
    return jax.shard_map(
        per_device, mesh=mesh, in_specs=in_specs, out_specs=out_specs, check_vma=False
    )
```

profile of v0, /device:TPU:2, one launch (start us, length us, event | category | flops | bytes accessed | tf_op | source)
XLA Modules:
  0.0 517.6 jit_solution(3128671705888314182)
XLA Ops:
  6.7 3.9 collective-permute-start.4
  18.8 5.2 %collective-permute-start.6 = (f32[8,10,1]{2,1,0:T(8,128)S(1)}, f32[8,10,1]{2,1,0:T(8,128)S(1)}, u32[]{:S(2)}, u32[]{:S(2)}) collective-permute-start(f32[8,10,1]{2,1,0:T(8,128)S(1)} %get-tuple-element.258), channel_id=1, source_target_pairs={{0,1},{1,2},{2,3},{4,5},{5,6},{6,7},{8,9},{9,10},{10,11},{12,13},{... | collective-permute-start | bytes 968 | tf_op jit(solution)/shard_map/ppermute | solution.py:22
  26.8 42.5 %all-reduce.13 = (f32[]{:T(128)}, f32[]{:T(128)}) all-reduce(f32[]{:T(128)} %get-tuple-element.13, f32[]{:T(128)} %get-tuple-element.12), channel_id=1, replica_groups=mesh['gx'=8,'sp'=4] {'gx','sp'}, use_global_device_ids=true, to_apply=%region_2.3 | all-reduce | flops 2 | bytes 16 | tf_op jit(solution)/shard_map/psum | solution.py:177
  72.7 3.6 collective-permute-start.9
  79.0 4.5 collective-permute-start.10
  86.4 42.6 %all-reduce.12 = (f32[]{:T(128)}, f32[]{:T(128)}) all-reduce(f32[]{:T(128)} %get-tuple-element.11, f32[]{:T(128)} %get-tuple-element.10), channel_id=1, replica_groups=mesh['gx'=8,'sp'=4] {'gx','sp'}, use_global_device_ids=true, to_apply=%region_7.8 | all-reduce | flops 2 | bytes 16 | tf_op jit(solution)/shard_map/psum | solution.py:177
  135.5 3.6 collective-permute-start.13
  142.0 4.5 collective-permute-start.14
  149.3 42.4 %all-reduce.11 = (f32[]{:T(128)}, f32[]{:T(128)}) all-reduce(f32[]{:T(128)} %get-tuple-element.9, f32[]{:T(128)} %get-tuple-element.8), channel_id=1, replica_groups=mesh['gx'=8,'sp'=4] {'gx','sp'}, use_global_device_ids=true, to_apply=%region_11.12 | all-reduce | flops 2 | bytes 16 | tf_op jit(solution)/shard_map/psum | solution.py:177
  197.6 3.6 collective-permute-start.17
  203.9 4.5 collective-permute-start.18
  211.3 42.3 %all-reduce.10 = (f32[]{:T(128)}, f32[]{:T(128)}) all-reduce(f32[]{:T(128)} %get-tuple-element.7, f32[]{:T(128)} %get-tuple-element.6), channel_id=1, replica_groups=mesh['gx'=8,'sp'=4] {'gx','sp'}, use_global_device_ids=true, to_apply=%region_15.16 | all-reduce | flops 2 | bytes 16 | tf_op jit(solution)/shard_map/psum | solution.py:177
  259.5 3.6 collective-permute-start.21
  265.8 4.5 collective-permute-start.22
  273.2 42.3 %all-reduce.9 = (f32[]{:T(128)}, f32[]{:T(128)}) all-reduce(f32[]{:T(128)} %get-tuple-element.5, f32[]{:T(128)} %get-tuple-element.4), channel_id=1, replica_groups=mesh['gx'=8,'sp'=4] {'gx','sp'}, use_global_device_ids=true, to_apply=%region_19.20 | all-reduce | flops 2 | bytes 16 | tf_op jit(solution)/shard_map/psum | solution.py:177
  328.3 4.5 collective-permute-start.26
  332.9 13.5 %all_gather.7 = f32[8,8,512]{2,1,0:T(8,128)S(1)} all-gather(f32[8,8,128]{2,1,0:T(8,128)S(1)} %get-tuple-element.14), channel_id=1, replica_groups=mesh['gx'=8,'sp'=4] {'sp'}, dimensions={2}, use_global_device_ids=true | all-gather | bytes 163840 | tf_op jit(solution)/shard_map/all_gather | solution.py:197
  347.3 39.6 %all-reduce.8 = (f32[]{:T(128)}, f32[]{:T(128)}) all-reduce(f32[]{:T(128)} %get-tuple-element.210, f32[]{:T(128)} %fusion.320), channel_id=1, replica_groups=mesh['gx'=8,'sp'=4] {'gx','sp'}, use_global_device_ids=true, to_apply=%region_23.24 | all-reduce | flops 2 | bytes 16 | tf_op jit(solution)/shard_map/psum | solution.py:177
  390.8 13.5 %all_gather.6 = f32[8,8,512]{2,1,0:T(8,128)S(1)} all-gather(f32[8,8,128]{2,1,0:T(8,128)S(1)} %multiply_add_fusion), channel_id=1, replica_groups=mesh['gx'=8,'sp'=4] {'sp'}, dimensions={2}, use_global_device_ids=true | all-gather | bytes 163840 | tf_op jit(solution)/shard_map/all_gather | solution.py:196
  406.5 14.5 %collective-permute-start.29 = (f32[5,8,1,512]{3,1,2,0:T(8,128)S(1)}, f32[5,8,1,512]{3,1,2,0:T(8,128)S(1)}, u32[]{:S(2)}, u32[]{:S(2)}) collective-permute-start(f32[5,8,1,512]{3,1,2,0:T(8,128)S(1)} %get-tuple-element.238), channel_id=1, source_target_pairs={{4,0},{8,4},{12,8},{16,12},{20,16},{24,20},{28,24},{5,1},{9,5},{13... | collective-permute-start | bytes 245768 | tf_op jit(solution)/shard_map/ppermute | solution.py:24
  424.1 4.1 copy.54
  428.2 6.1 %reshape.95 = f32[4,1,24576]{2,1,0:T(1,128)} reshape(f32[512,3,8,8]{3,2,1,0:T(8,128)} %bitcast.69) | data formatting | bytes 786432
  438.2 11.8 %all-to-all-done = f32[4,1,24576]{2,1,0:T(1,128)S(1)} async-done(((f32[4,1,24576]{2,1,0:T(1,128)}), f32[4,1,24576]{2,1,0:T(1,128)S(1)}, u32[]{:S(2)}, u32[]{:S(2)}) %all-to-all-start) | async-done | bytes 393248 | tf_op jit(solution)/shard_map/all_to_all | solution.py:145
  452.3 6.2 %reshape.96 = f32[512,3,8,8]{3,2,1,0:T(8,128)} reshape(f32[4,24576]{1,0:T(4,128)S(1)} %reduce) | data formatting | bytes 786432
  458.5 4.3 copy.55
  464.0 3.9 convolution_multiply_fusion.1
  467.9 7.2 %subtract_multiply_fusion.64 = (f32[1,8192]{1,0:T(1,128)S(1)}, f32[1,8192]{1,0:T(1,128)S(1)}, f32[1,8192]{1,0:T(1,128)S(1)}, f32[1,8192]{1,0:T(1,128)S(1)}, f32[...) fusion(f32[12,8192]{1,0:T(8,128)S(1)} %fusion.3, ...), kind=kLoop, calls=%fused_computation.862 | loop fusion | flops 5136384 | bytes 4751360 | tf_op jit(solution)/shard_map/mul | solution.py:94
  478.1 4.1 subtract_multiply_fusion.46
  484.1 3.9 convolution_multiply_fusion
  488.0 7.3 %subtract_multiply_fusion.18 = (f32[1,8192]{1,0:T(1,128)S(1)}, f32[1,8192]{1,0:T(1,128)S(1)}, f32[1,8192]{1,0:T(1,128)S(1)}, f32[1,8192]{1,0:T(1,128)S(1)}, f32[...) fusion(f32[12,8192]{1,0:T(8,128)S(1)} %fusion.1, ...), kind=kLoop, calls=%fused_computation.808 | loop fusion | flops 5136384 | bytes 4751360 | tf_op jit(solution)/shard_map/mul | solution.py:94
  498.0 4.1 subtract_multiply_fusion
  502.5 13.9 %all_to_all.33 = f32[12,8,8,128]{3,2,1,0:T(8,128)S(1)} all-to-all(f32[12,8,8,128]{3,2,1,0:T(8,128)S(1)} %fusion.11), channel_id=1, replica_groups=mesh['gx'=8,'sp'=4] {'sp'}, dimensions={0} | all-to-all | bytes 786432 | tf_op jit(solution)/shard_map/all_to_all | solution.py:209
  (153 shorter events, 77.6 us)
Async XLA Ops:
  1.5 11.0 %collective-permute-start.1 = (f32[8,1,128]{2,1,0:T(1,128)S(1)}, f32[8,1,128]{2,1,0:T(1,128)S(1)}, u32[]{:S(2)}, u32[]{:S(2)}) collective-permute-start(f32[8,1,128]{2,1,0:T(1,128)S(1)} %get-tuple-element.269), channel_id=1, source_target_pairs={{4,0},{8,4},{12,8},{16,12},{20,16},{24,20},{28,24},{5,1},{9,5},{13... | collective-permute-start | bytes 12296 | tf_op jit(solution)/shard_map/ppermute | solution.py:24
  3.5 9.0 %collective-permute-start = (f32[8,1,128]{2,1,0:T(1,128)S(1)}, f32[8,1,128]{2,1,0:T(1,128)S(1)}, u32[]{:S(2)}, u32[]{:S(2)}) collective-permute-start(f32[8,1,128]{2,1,0:T(1,128)S(1)} %get-tuple-element.270), channel_id=1, source_target_pairs={{0,4},{4,8},{8,12},{12,16},{16,20},{20,24},{24,28},{1,5},{5,9},{9,... | collective-permute-start | bytes 12296 | tf_op jit(solution)/shard_map/ppermute | solution.py:22
  6.7 10.7 %collective-permute-start.4 = (f32[8,1,128]{2,1,0:T(1,128)S(1)}, f32[8,1,128]{2,1,0:T(1,128)S(1)}, u32[]{:S(2)}, u32[]{:S(2)}) collective-permute-start(f32[8,1,128]{2,1,0:T(1,128)S(1)} %get-tuple-element.271), channel_id=1, source_target_pairs={{0,4},{4,8},{8,12},{12,16},{16,20},{20,24},{24,28},{1,5},{5,9},{9,... | collective-permute-start | bytes 12296 | tf_op jit(solution)/shard_map/ppermute | solution.py:22
  10.5 6.9 %collective-permute-start.5 = (f32[8,1,128]{2,1,0:T(1,128)S(1)}, f32[8,1,128]{2,1,0:T(1,128)S(1)}, u32[]{:S(2)}, u32[]{:S(2)}) collective-permute-start(f32[8,1,128]{2,1,0:T(1,128)S(1)} %get-tuple-element.272), channel_id=1, source_target_pairs={{4,0},{8,4},{12,8},{16,12},{20,16},{24,20},{28,24},{5,1},{9,5},{13... | collective-permute-start | bytes 12296 | tf_op jit(solution)/shard_map/ppermute | solution.py:24
  12.6 11.4 %collective-permute-start.2 = (f32[8,10,1]{2,1,0:T(8,128)S(1)}, f32[8,10,1]{2,1,0:T(8,128)S(1)}, u32[]{:S(2)}, u32[]{:S(2)}) collective-permute-start(f32[8,10,1]{2,1,0:T(8,128)S(1)} %get-tuple-element.255), channel_id=1, source_target_pairs={{0,1},{1,2},{2,3},{4,5},{5,6},{6,7},{8,9},{9,10},{10,11},{12,13},{... | collective-permute-start | bytes 968 | tf_op jit(solution)/shard_map/ppermute | solution.py:22
  16.1 7.9 %collective-permute-start.3 = (f32[8,10,1]{2,1,0:T(8,128)S(1)}, f32[8,10,1]{2,1,0:T(8,128)S(1)}, u32[]{:S(2)}, u32[]{:S(2)}) collective-permute-start(f32[8,10,1]{2,1,0:T(8,128)S(1)} %get-tuple-element.256), channel_id=1, source_target_pairs={{1,0},{2,1},{3,2},{5,4},{6,5},{7,6},{9,8},{10,9},{11,10},{13,12},{... | collective-permute-start | bytes 968 | tf_op jit(solution)/shard_map/ppermute | solution.py:24
  17.5 6.8 %collective-permute-start.7 = (f32[8,10,1]{2,1,0:T(8,128)S(1)}, f32[8,10,1]{2,1,0:T(8,128)S(1)}, u32[]{:S(2)}, u32[]{:S(2)}) collective-permute-start(f32[8,10,1]{2,1,0:T(8,128)S(1)} %get-tuple-element.257), channel_id=1, source_target_pairs={{1,0},{2,1},{3,2},{5,4},{6,5},{7,6},{9,8},{10,9},{11,10},{13,12},{... | collective-permute-start | bytes 968 | tf_op jit(solution)/shard_map/ppermute | solution.py:24
  18.8 7.1 %collective-permute-start.6 = (f32[8,10,1]{2,1,0:T(8,128)S(1)}, f32[8,10,1]{2,1,0:T(8,128)S(1)}, u32[]{:S(2)}, u32[]{:S(2)}) collective-permute-start(f32[8,10,1]{2,1,0:T(8,128)S(1)} %get-tuple-element.258), channel_id=1, source_target_pairs={{0,1},{1,2},{2,3},{4,5},{5,6},{6,7},{8,9},{9,10},{10,11},{12,13},{... | collective-permute-start | bytes 968 | tf_op jit(solution)/shard_map/ppermute | solution.py:22
  70.7 5.6 %collective-permute-start.8 = (f32[8,1,128]{2,1,0:T(1,128)S(1)}, f32[8,1,128]{2,1,0:T(1,128)S(1)}, u32[]{:S(2)}, u32[]{:S(2)}) collective-permute-start(f32[8,1,128]{2,1,0:T(1,128)S(1)} %get-tuple-element.267), channel_id=1, source_target_pairs={{0,4},{4,8},{8,12},{12,16},{16,20},{20,24},{24,28},{1,5},{5,9},{9,... | collective-permute-start | bytes 12296 | tf_op jit(solution)/shard_map/ppermute | solution.py:22
  72.7 5.0 collective-permute-start.9
  77.7 6.2 %collective-permute-start.11 = (f32[8,10,1]{2,1,0:T(8,128)S(1)}, f32[8,10,1]{2,1,0:T(8,128)S(1)}, u32[]{:S(2)}, u32[]{:S(2)}) collective-permute-start(f32[8,10,1]{2,1,0:T(8,128)S(1)} %get-tuple-element.253), channel_id=1, source_target_pairs={{1,0},{2,1},{3,2},{5,4},{6,5},{7,6},{9,8},{10,9},{11,10},{13,12},{... | collective-permute-start | bytes 968 | tf_op jit(solution)/shard_map/ppermute | solution.py:24
  79.0 6.4 %collective-permute-start.10 = (f32[8,10,1]{2,1,0:T(8,128)S(1)}, f32[8,10,1]{2,1,0:T(8,128)S(1)}, u32[]{:S(2)}, u32[]{:S(2)}) collective-permute-start(f32[8,10,1]{2,1,0:T(8,128)S(1)} %get-tuple-element.254), channel_id=1, source_target_pairs={{0,1},{1,2},{2,3},{4,5},{5,6},{6,7},{8,9},{9,10},{10,11},{12,13},{... | collective-permute-start | bytes 968 | tf_op jit(solution)/shard_map/ppermute | solution.py:22
  133.6 5.6 %collective-permute-start.12 = (f32[8,1,128]{2,1,0:T(1,128)S(1)}, f32[8,1,128]{2,1,0:T(1,128)S(1)}, u32[]{:S(2)}, u32[]{:S(2)}) collective-permute-start(f32[8,1,128]{2,1,0:T(1,128)S(1)} %get-tuple-element.265), channel_id=1, source_target_pairs={{0,4},{4,8},{8,12},{12,16},{16,20},{20,24},{24,28},{1,5},{5,9},{9,... | collective-permute-start | bytes 12296 | tf_op jit(solution)/shard_map/ppermute | solution.py:22
  135.5 5.0 collective-permute-start.13
  140.5 185.2 %copy-start = (f32[3,8,8,512]{3,2,1,0:T(8,128)S(1)}, f32[3,8,8,512]{3,2,1,0:T(8,128)}, u32[]{:S(2)}) copy-start(f32[3,8,8,512]{3,2,1,0:T(8,128)} %param.15) | copy-start | bytes 1179652
  140.6 6.3 %collective-permute-start.15 = (f32[8,10,1]{2,1,0:T(8,128)S(1)}, f32[8,10,1]{2,1,0:T(8,128)S(1)}, u32[]{:S(2)}, u32[]{:S(2)}) collective-permute-start(f32[8,10,1]{2,1,0:T(8,128)S(1)} %get-tuple-element.251), channel_id=1, source_target_pairs={{1,0},{2,1},{3,2},{5,4},{6,5},{7,6},{9,8},{10,9},{11,10},{13,12},{... | collective-permute-start | bytes 968 | tf_op jit(solution)/shard_map/ppermute | solution.py:24
  142.0 6.4 %collective-permute-start.14 = (f32[8,10,1]{2,1,0:T(8,128)S(1)}, f32[8,10,1]{2,1,0:T(8,128)S(1)}, u32[]{:S(2)}, u32[]{:S(2)}) collective-permute-start(f32[8,10,1]{2,1,0:T(8,128)S(1)} %get-tuple-element.252), channel_id=1, source_target_pairs={{0,1},{1,2},{2,3},{4,5},{5,6},{6,7},{8,9},{9,10},{10,11},{12,13},{... | collective-permute-start | bytes 968 | tf_op jit(solution)/shard_map/ppermute | solution.py:22
  195.7 5.6 %collective-permute-start.16 = (f32[8,1,128]{2,1,0:T(1,128)S(1)}, f32[8,1,128]{2,1,0:T(1,128)S(1)}, u32[]{:S(2)}, u32[]{:S(2)}) collective-permute-start(f32[8,1,128]{2,1,0:T(1,128)S(1)} %get-tuple-element.263), channel_id=1, source_target_pairs={{0,4},{4,8},{8,12},{12,16},{16,20},{20,24},{24,28},{1,5},{5,9},{9,... | collective-permute-start | bytes 12296 | tf_op jit(solution)/shard_map/ppermute | solution.py:22
  197.6 5.0 collective-permute-start.17
  202.7 6.2 %collective-permute-start.19 = (f32[8,10,1]{2,1,0:T(8,128)S(1)}, f32[8,10,1]{2,1,0:T(8,128)S(1)}, u32[]{:S(2)}, u32[]{:S(2)}) collective-permute-start(f32[8,10,1]{2,1,0:T(8,128)S(1)} %get-tuple-element.249), channel_id=1, source_target_pairs={{1,0},{2,1},{3,2},{5,4},{6,5},{7,6},{9,8},{10,9},{11,10},{13,12},{... | collective-permute-start | bytes 968 | tf_op jit(solution)/shard_map/ppermute | solution.py:24
  203.9 6.4 %collective-permute-start.18 = (f32[8,10,1]{2,1,0:T(8,128)S(1)}, f32[8,10,1]{2,1,0:T(8,128)S(1)}, u32[]{:S(2)}, u32[]{:S(2)}) collective-permute-start(f32[8,10,1]{2,1,0:T(8,128)S(1)} %get-tuple-element.250), channel_id=1, source_target_pairs={{0,1},{1,2},{2,3},{4,5},{5,6},{6,7},{8,9},{9,10},{10,11},{12,13},{... | collective-permute-start | bytes 968 | tf_op jit(solution)/shard_map/ppermute | solution.py:22
  257.6 5.6 %collective-permute-start.20 = (f32[8,1,128]{2,1,0:T(1,128)S(1)}, f32[8,1,128]{2,1,0:T(1,128)S(1)}, u32[]{:S(2)}, u32[]{:S(2)}) collective-permute-start(f32[8,1,128]{2,1,0:T(1,128)S(1)} %get-tuple-element.261), channel_id=1, source_target_pairs={{0,4},{4,8},{8,12},{12,16},{16,20},{20,24},{24,28},{1,5},{5,9},{9,... | collective-permute-start | bytes 12296 | tf_op jit(solution)/shard_map/ppermute | solution.py:22
  259.5 5.0 collective-permute-start.21
  264.5 6.2 %collective-permute-start.23 = (f32[8,10,1]{2,1,0:T(8,128)S(1)}, f32[8,10,1]{2,1,0:T(8,128)S(1)}, u32[]{:S(2)}, u32[]{:S(2)}) collective-permute-start(f32[8,10,1]{2,1,0:T(8,128)S(1)} %get-tuple-element.247), channel_id=1, source_target_pairs={{1,0},{2,1},{3,2},{5,4},{6,5},{7,6},{9,8},{10,9},{11,10},{13,12},{... | collective-permute-start | bytes 968 | tf_op jit(solution)/shard_map/ppermute | solution.py:24
  265.8 6.4 %collective-permute-start.22 = (f32[8,10,1]{2,1,0:T(8,128)S(1)}, f32[8,10,1]{2,1,0:T(8,128)S(1)}, u32[]{:S(2)}, u32[]{:S(2)}) collective-permute-start(f32[8,10,1]{2,1,0:T(8,128)S(1)} %get-tuple-element.248), channel_id=1, source_target_pairs={{0,1},{1,2},{2,3},{4,5},{5,6},{6,7},{8,9},{9,10},{10,11},{12,13},{... | collective-permute-start | bytes 968 | tf_op jit(solution)/shard_map/ppermute | solution.py:22
  320.1 5.8 %collective-permute-start.24 = (f32[8,1,128]{2,1,0:T(1,128)S(1)}, f32[8,1,128]{2,1,0:T(1,128)S(1)}, u32[]{:S(2)}, u32[]{:S(2)}) collective-permute-start(f32[8,1,128]{2,1,0:T(1,128)S(1)} %get-tuple-element.259), channel_id=1, source_target_pairs={{0,4},{4,8},{8,12},{12,16},{16,20},{20,24},{24,28},{1,5},{5,9},{9,... | collective-permute-start | bytes 12296 | tf_op jit(solution)/shard_map/ppermute | solution.py:22
  322.0 5.0 collective-permute-start.25
  327.1 19.3 %collective-permute-start.27 = (f32[8,10,1]{2,1,0:T(8,128)S(1)}, f32[8,10,1]{2,1,0:T(8,128)S(1)}, u32[]{:S(2)}, u32[]{:S(2)}) collective-permute-start(f32[8,10,1]{2,1,0:T(8,128)S(1)} %get-tuple-element.245), channel_id=1, source_target_pairs={{1,0},{2,1},{3,2},{5,4},{6,5},{7,6},{9,8},{10,9},{11,10},{13,12},{... | collective-permute-start | bytes 968 | tf_op jit(solution)/shard_map/ppermute | solution.py:24
  328.3 18.0 %collective-permute-start.26 = (f32[8,10,1]{2,1,0:T(8,128)S(1)}, f32[8,10,1]{2,1,0:T(8,128)S(1)}, u32[]{:S(2)}, u32[]{:S(2)}) collective-permute-start(f32[8,10,1]{2,1,0:T(8,128)S(1)} %get-tuple-element.246), channel_id=1, source_target_pairs={{0,1},{1,2},{2,3},{4,5},{5,6},{6,7},{8,9},{9,10},{10,11},{12,13},{... | collective-permute-start | bytes 968 | tf_op jit(solution)/shard_map/ppermute | solution.py:22
  404.6 16.4 %collective-permute-start.28 = (f32[5,8,1,512]{3,1,2,0:T(8,128)S(1)}, f32[5,8,1,512]{3,1,2,0:T(8,128)S(1)}, u32[]{:S(2)}, u32[]{:S(2)}) collective-permute-start(f32[5,8,1,512]{3,1,2,0:T(8,128)S(1)} %get-tuple-element.237), channel_id=1, source_target_pairs={{0,4},{4,8},{8,12},{12,16},{16,20},{20,24},{24,28},{1,5},{5,9},{9,... | collective-permute-start | bytes 245768 | tf_op jit(solution)/shard_map/ppermute | solution.py:22
  406.5 14.5 %collective-permute-start.29 = (f32[5,8,1,512]{3,1,2,0:T(8,128)S(1)}, f32[5,8,1,512]{3,1,2,0:T(8,128)S(1)}, u32[]{:S(2)}, u32[]{:S(2)}) collective-permute-start(f32[5,8,1,512]{3,1,2,0:T(8,128)S(1)} %get-tuple-element.238), channel_id=1, source_target_pairs={{4,0},{8,4},{12,8},{16,12},{20,16},{24,20},{28,24},{5,1},{9,5},{13... | collective-permute-start | bytes 245768 | tf_op jit(solution)/shard_map/ppermute | solution.py:24
  434.2 15.8 %all-to-all-start = ((f32[4,1,24576]{2,1,0:T(1,128)}), f32[4,1,24576]{2,1,0:T(1,128)S(1)}, u32[]{:S(2)}, u32[]{:S(2)}) async-start(f32[4,1,24576]{2,1,0:T(1,128)} %reshape.95), calls=%async_computation | async-start | bytes 786432 | tf_op jit(solution)/shard_map/all_to_all | solution.py:145
  (5 other events, 64.3 us)
where the time goes:
time: 527 us; the launch traced here: 518 us
  blocking collectives  293 us (56%)
  starting transfers between devices  98.3 us (19%)
  other arithmetic  41.7 us (8%)
  waiting for transfers between devices  27.3 us (5%)
  local copies, waits for them, and re-layouts  24 us (5%)
  between operations  23.5 us (4%)
  matrix products  10.1 us (2%)
    psum x6, blocking collectives, inner_pair(): lax.psum((jnp.sum(first * first), jnp.sum(first * second)), ('gx', 'sp'))  252 us
    ppermute x15, starting transfers between devices, padded_2(): lax.ppermute(tail, axis, [(i, (i + 1) % count) for i in range(ends)])  49.2 us
    ppermute x15, starting transfers between devices, padded_2(): lax.ppermute(head, axis, [((i + 1) % count, i) for i in range(ends)])  45.7 us
    mul x2, other arithmetic, solve_system(): forward.append(running * inverse[i])  14.5 us
    all_to_all x1, blocking collectives, per_device(): lax.all_to_all(reacted, 'sp', split_axis=0, concat_axis=3, tiled=True)  13.9 us
    all_gather x1, blocking collectives, per_device(): lax.all_gather(head_field, 'sp', axis=2, tiled=True)  13.5 us
    all_gather x1, blocking collectives, per_device(): lax.all_gather(conduct, 'sp', axis=2, tiled=True)  13.5 us
    unnamed x38, local copies, waits for them, and re-layouts  12.7 us
  transfers between devices with their start and end apart: 31, of which 16 were waited for; matrix products, arithmetic and copies ran while one was open for 0% of the time, Pallas kernels for 0%

commit v1 on v0

--- a/solution.py
+++ b/solution.py
@@ -174,7 +174,7 @@
     residual = source
 
     def inner_pair(first, second):
-        return lax.psum((jnp.sum(first * first), jnp.sum(first * second)), ("gx", "sp"))
+        return lax.psum(lax.psum((jnp.sum(first * first), jnp.sum(first * second)), "gx"), "sp")
 
     image = operate(residual)
     norm_now, product = inner_pair(residual, image)

time: 527 us -> 411 us (0.78); the launches traced: 518 us -> 409 us
  blocking collectives: 293 us -> 187 us
  starting transfers between devices: 98.3 us -> 87.7 us
  waiting for transfers between devices: 27.3 us -> 35.8 us
    psum x6 -> x12, blocking collectives: 252 us -> 143 us  [the longest x6 75.3 us: inner_pair(): lax.psum((jnp.sum(first * first), jnp.sum(first * second)), 'gx')]
    ppermute x15, starting transfers between devices: 45.7 us -> 34.8 us  [padded_2(): lax.ppermute(head, axis, [((i + 1) % count, i) for i in range(ends)])]
    ppermute x15, waiting for transfers between devices: 7.58 us -> 18.3 us  [padded_2(): lax.ppermute(head, axis, [((i + 1) % count, i) for i in range(ends)])]
  transfers between devices with their start and end apart: 31 -> 31, of which waited for: 16 -> 18; matrix products, arithmetic and copies ran while one was open for 0% -> 0% of each run, Pallas kernels for 0% -> 0%
where the time goes in v1:
time: 411 us; the launch traced here: 409 us
  blocking collectives  187 us (45%)
  starting transfers between devices  87.7 us (21%)
  other arithmetic  41.9 us (10%)
  waiting for transfers between devices  35.8 us (9%)
  local copies, waits for them, and re-layouts  24 us (6%)
  between operations  23.1 us (6%)
  matrix products  10.1 us (2%)
    psum x6, blocking collectives, inner_pair(): lax.psum((jnp.sum(first * first), jnp.sum(first * second)), 'gx')  75.3 us
    psum x6, blocking collectives, inner_pair(): lax.psum(lax.psum((jnp.sum(first * first), jnp.sum(first * second)), 'gx'...  67.3 us
    ppermute x15, starting transfers between devices, padded_2(): lax.ppermute(tail, axis, [(i, (i + 1) % count) for i in range(ends)])  49.2 us
    ppermute x15, starting transfers between devices, padded_2(): lax.ppermute(head, axis, [((i + 1) % count, i) for i in range(ends)])  34.8 us
    ppermute x15, waiting for transfers between devices, padded_2(): lax.ppermute(head, axis, [((i + 1) % count, i) for i in range(ends)])  18.3 us
    all_to_all x1, blocking collectives, per_device(): lax.all_to_all(reacted, 'sp', split_axis=0, concat_axis=3, tiled=True)  17.4 us
    mul x2, other arithmetic, solve_system(): forward.append(running * inverse[i])  14.5 us
    all_gather x1, blocking collectives, per_device(): lax.all_gather(conduct, 'sp', axis=2, tiled=True)  13.6 us
  transfers between devices with their start and end apart: 31, of which 18 were waited for; matrix products, arithmetic and copies ran while one was open for 0% of the time, Pallas kernels for 0%

profile of v1, /device:TPU:2, one launch (start us, length us, event | category | flops | bytes accessed | tf_op | source)
XLA Modules:
  0.0 409.5 jit_solution(17676106246976844474)
XLA Ops:
  18.8 5.2 %collective-permute-start.6 = (f32[8,10,1]{2,1,0:T(8,128)S(1)}, f32[8,10,1]{2,1,0:T(8,128)S(1)}, u32[]{:S(2)}, u32[]{:S(2)}) collective-permute-start(f32[8,10,1]{2,1,0:T(8,128)S(1)} %get-tuple-element.270), channel_id=1, source_target_pairs={{0,1},{1,2},{2,3},{4,5},{5,6},{6,7},{8,9},{9,10},{10,11},{12,13},{... | collective-permute-start | bytes 968 | tf_op jit(solution)/shard_map/ppermute | solution.py:22
  26.8 11.3 %all-reduce.13 = (f32[]{:T(128)}, f32[]{:T(128)}) all-reduce(f32[]{:T(128)} %get-tuple-element.13, f32[]{:T(128)} %get-tuple-element.12), channel_id=1, replica_groups=mesh['gx'=8,'sp'=4] {'gx'}, use_global_device_ids=true, to_apply=%region_2.3 | all-reduce | flops 2 | bytes 16 | tf_op jit(solution)/shard_map/psum | solution.py:177
  38.2 13.8 %all-reduce.19 = (f32[]{:T(128)}, f32[]{:T(128)}) all-reduce(f32[]{:T(128)} %get-tuple-element.26, f32[]{:T(128)} %get-tuple-element.27), channel_id=1, replica_groups=mesh['gx'=8,'sp'=4] {'sp'}, use_global_device_ids=true, to_apply=%region_3.4 | all-reduce | flops 2 | bytes 16 | tf_op jit(solution)/shard_map/psum | solution.py:177
  63.0 4.5 %collective-permute-start.10 = (f32[8,10,1]{2,1,0:T(8,128)S(1)}, f32[8,10,1]{2,1,0:T(8,128)S(1)}, u32[]{:S(2)}, u32[]{:S(2)}) collective-permute-start(f32[8,10,1]{2,1,0:T(8,128)S(1)} %get-tuple-element.266), channel_id=1, source_target_pairs={{0,1},{1,2},{2,3},{4,5},{5,6},{6,7},{8,9},{9,10},{10,11},{12,13},{... | collective-permute-start | bytes 968 | tf_op jit(solution)/shard_map/ppermute | solution.py:22
  70.4 13.1 %all-reduce.12 = (f32[]{:T(128)}, f32[]{:T(128)}) all-reduce(f32[]{:T(128)} %get-tuple-element.11, f32[]{:T(128)} %get-tuple-element.10), channel_id=1, replica_groups=mesh['gx'=8,'sp'=4] {'gx'}, use_global_device_ids=true, to_apply=%region_9.10 | all-reduce | flops 2 | bytes 16 | tf_op jit(solution)/shard_map/psum | solution.py:177
  83.4 11.1 %all-reduce.18 = (f32[]{:T(128)}, f32[]{:T(128)}) all-reduce(f32[]{:T(128)} %get-tuple-element.24, f32[]{:T(128)} %get-tuple-element.25), channel_id=1, replica_groups=mesh['gx'=8,'sp'=4] {'sp'}, use_global_device_ids=true, to_apply=%region_10.11 | all-reduce | flops 2 | bytes 16 | tf_op jit(solution)/shard_map/psum | solution.py:177
  109.2 4.5 %collective-permute-start.14 = (f32[8,10,1]{2,1,0:T(8,128)S(1)}, f32[8,10,1]{2,1,0:T(8,128)S(1)}, u32[]{:S(2)}, u32[]{:S(2)}) collective-permute-start(f32[8,10,1]{2,1,0:T(8,128)S(1)} %get-tuple-element.264), channel_id=1, source_target_pairs={{0,1},{1,2},{2,3},{4,5},{5,6},{6,7},{8,9},{9,10},{10,11},{12,13},{... | collective-permute-start | bytes 968 | tf_op jit(solution)/shard_map/ppermute | solution.py:22
  116.5 13.0 %all-reduce.11 = (f32[]{:T(128)}, f32[]{:T(128)}) all-reduce(f32[]{:T(128)} %get-tuple-element.9, f32[]{:T(128)} %get-tuple-element.8), channel_id=1, replica_groups=mesh['gx'=8,'sp'=4] {'gx'}, use_global_device_ids=true, to_apply=%region_15.16 | all-reduce | flops 2 | bytes 16 | tf_op jit(solution)/shard_map/psum | solution.py:177
  129.5 11.1 %all-reduce.17 = (f32[]{:T(128)}, f32[]{:T(128)}) all-reduce(f32[]{:T(128)} %get-tuple-element.22, f32[]{:T(128)} %get-tuple-element.23), channel_id=1, replica_groups=mesh['gx'=8,'sp'=4] {'sp'}, use_global_device_ids=true, to_apply=%region_16.17 | all-reduce | flops 2 | bytes 16 | tf_op jit(solution)/shard_map/psum | solution.py:177
  154.5 4.5 %collective-permute-start.18 = (f32[8,10,1]{2,1,0:T(8,128)S(1)}, f32[8,10,1]{2,1,0:T(8,128)S(1)}, u32[]{:S(2)}, u32[]{:S(2)}) collective-permute-start(f32[8,10,1]{2,1,0:T(8,128)S(1)} %get-tuple-element.262), channel_id=1, source_target_pairs={{0,1},{1,2},{2,3},{4,5},{5,6},{6,7},{8,9},{9,10},{10,11},{12,13},{... | collective-permute-start | bytes 968 | tf_op jit(solution)/shard_map/ppermute | solution.py:22
  162.0 13.0 %all-reduce.10 = (f32[]{:T(128)}, f32[]{:T(128)}) all-reduce(f32[]{:T(128)} %get-tuple-element.7, f32[]{:T(128)} %get-tuple-element.6), channel_id=1, replica_groups=mesh['gx'=8,'sp'=4] {'gx'}, use_global_device_ids=true, to_apply=%region_21.22 | all-reduce | flops 2 | bytes 16 | tf_op jit(solution)/shard_map/psum | solution.py:177
  175.0 11.2 %all-reduce.16 = (f32[]{:T(128)}, f32[]{:T(128)}) all-reduce(f32[]{:T(128)} %get-tuple-element.20, f32[]{:T(128)} %get-tuple-element.21), channel_id=1, replica_groups=mesh['gx'=8,'sp'=4] {'sp'}, use_global_device_ids=true, to_apply=%region_22.23 | all-reduce | flops 2 | bytes 16 | tf_op jit(solution)/shard_map/psum | solution.py:177
  200.1 4.5 %collective-permute-start.22 = (f32[8,10,1]{2,1,0:T(8,128)S(1)}, f32[8,10,1]{2,1,0:T(8,128)S(1)}, u32[]{:S(2)}, u32[]{:S(2)}) collective-permute-start(f32[8,10,1]{2,1,0:T(8,128)S(1)} %get-tuple-element.260), channel_id=1, source_target_pairs={{0,1},{1,2},{2,3},{4,5},{5,6},{6,7},{8,9},{9,10},{10,11},{12,13},{... | collective-permute-start | bytes 968 | tf_op jit(solution)/shard_map/ppermute | solution.py:22
  207.4 13.0 %all-reduce.9 = (f32[]{:T(128)}, f32[]{:T(128)}) all-reduce(f32[]{:T(128)} %get-tuple-element.5, f32[]{:T(128)} %get-tuple-element.4), channel_id=1, replica_groups=mesh['gx'=8,'sp'=4] {'gx'}, use_global_device_ids=true, to_apply=%region_27.28 | all-reduce | flops 2 | bytes 16 | tf_op jit(solution)/shard_map/psum | solution.py:177
  220.4 11.1 %all-reduce.15 = (f32[]{:T(128)}, f32[]{:T(128)}) all-reduce(f32[]{:T(128)} %get-tuple-element.18, f32[]{:T(128)} %get-tuple-element.19), channel_id=1, replica_groups=mesh['gx'=8,'sp'=4] {'sp'}, use_global_device_ids=true, to_apply=%region_28.29 | all-reduce | flops 2 | bytes 16 | tf_op jit(solution)/shard_map/psum | solution.py:177
  246.1 4.5 %collective-permute-start.26 = (f32[8,10,1]{2,1,0:T(8,128)S(1)}, f32[8,10,1]{2,1,0:T(8,128)S(1)}, u32[]{:S(2)}, u32[]{:S(2)}) collective-permute-start(f32[8,10,1]{2,1,0:T(8,128)S(1)} %get-tuple-element.258), channel_id=1, source_target_pairs={{0,1},{1,2},{2,3},{4,5},{5,6},{6,7},{8,9},{9,10},{10,11},{12,13},{... | collective-permute-start | bytes 968 | tf_op jit(solution)/shard_map/ppermute | solution.py:22
  250.6 13.6 %all_gather.7 = f32[8,8,512]{2,1,0:T(8,128)S(1)} all-gather(f32[8,8,128]{2,1,0:T(8,128)S(1)} %get-tuple-element.14), channel_id=1, replica_groups=mesh['gx'=8,'sp'=4] {'sp'}, dimensions={2}, use_global_device_ids=true | all-gather | bytes 163840 | tf_op jit(solution)/shard_map/all_gather | solution.py:197
  265.2 11.8 %all-reduce.8 = (f32[]{:T(128)}, f32[]{:T(128)}) all-reduce(f32[]{:T(128)} %get-tuple-element.222, f32[]{:T(128)} %fusion.320), channel_id=1, replica_groups=mesh['gx'=8,'sp'=4] {'gx'}, use_global_device_ids=true, to_apply=%region_33.34 | all-reduce | flops 2 | bytes 16 | tf_op jit(solution)/shard_map/psum | solution.py:177
  277.1 9.0 %all-reduce.14 = (f32[]{:T(128)}, f32[]{:T(128)}) all-reduce(f32[]{:T(128)} %get-tuple-element.16, f32[]{:T(128)} %get-tuple-element.17), channel_id=1, replica_groups=mesh['gx'=8,'sp'=4] {'sp'}, use_global_device_ids=true, to_apply=%region_34.35 | all-reduce | flops 2 | bytes 16 | tf_op jit(solution)/shard_map/psum | solution.py:177
  290.1 13.4 %all_gather.6 = f32[8,8,512]{2,1,0:T(8,128)S(1)} all-gather(f32[8,8,128]{2,1,0:T(8,128)S(1)} %multiply_add_fusion), channel_id=1, replica_groups=mesh['gx'=8,'sp'=4] {'sp'}, dimensions={2}, use_global_device_ids=true | all-gather | bytes 163840 | tf_op jit(solution)/shard_map/all_gather | solution.py:196
  315.1 4.1 copy.54
  319.2 6.1 %reshape.95 = f32[4,1,24576]{2,1,0:T(1,128)} reshape(f32[512,3,8,8]{3,2,1,0:T(8,128)} %bitcast.69) | data formatting | bytes 786432
  329.4 9.3 %all-to-all-done = f32[4,1,24576]{2,1,0:T(1,128)S(1)} async-done(((f32[4,1,24576]{2,1,0:T(1,128)}), f32[4,1,24576]{2,1,0:T(1,128)S(1)}, u32[]{:S(2)}, u32[]{:S(2)}) %all-to-all-start) | async-done | bytes 393248 | tf_op jit(solution)/shard_map/all_to_all | solution.py:145
  341.0 6.2 %reshape.96 = f32[512,3,8,8]{3,2,1,0:T(8,128)} reshape(f32[4,24576]{1,0:T(4,128)S(1)} %reduce) | data formatting | bytes 786432
  347.2 4.3 %copy.55 = f32[3,8,8,4,128]{4,2,1,0,3:T(8,128)S(1)} copy(f32[3,8,8,4,128]{2,1,0,4,3:T(8,128)} %bitcast.70) | data formatting | bytes 786432 | tf_op jit(solution)/shard_map/all_to_all | solution.py:145
  352.8 3.9 convolution_multiply_fusion.1
  356.7 7.2 %subtract_multiply_fusion.64 = (f32[1,8192]{1,0:T(1,128)S(1)}, f32[1,8192]{1,0:T(1,128)S(1)}, f32[1,8192]{1,0:T(1,128)S(1)}, f32[1,8192]{1,0:T(1,128)S(1)}, f32[...) fusion(f32[12,8192]{1,0:T(8,128)S(1)} %fusion.3, ...), kind=kLoop, calls=%fused_computation.862 | loop fusion | flops 5136384 | bytes 4751360 | tf_op jit(solution)/shard_map/mul | solution.py:94
  366.9 4.1 %subtract_multiply_fusion.46 = (f32[1,8192]{1,0:T(1,128)S(1)}, f32[1,8192]{1,0:T(1,128)S(1)}, f32[1,8192]{1,0:T(1,128)S(1)}, f32[1,8192]{1,0:T(1,128)S(1)}, f32[...) fusion(f32[1,8192]{1,0:T(1,128)S(1)} %get-tuple-element.221, ...), kind=kLoop, calls=%fused_computation.843 | loop fusion | flops 2220032 | bytes 3342336 | tf_op jit(solution)/shard_map/mul | solution.py:100
  372.9 3.9 convolution_multiply_fusion
  376.8 7.3 %subtract_multiply_fusion.18 = (f32[1,8192]{1,0:T(1,128)S(1)}, f32[1,8192]{1,0:T(1,128)S(1)}, f32[1,8192]{1,0:T(1,128)S(1)}, f32[1,8192]{1,0:T(1,128)S(1)}, f32[...) fusion(f32[12,8192]{1,0:T(8,128)S(1)} %fusion.1, ...), kind=kLoop, calls=%fused_computation.808 | loop fusion | flops 5136384 | bytes 4751360 | tf_op jit(solution)/shard_map/mul | solution.py:94
  386.8 4.1 %subtract_multiply_fusion = (f32[1,8192]{1,0:T(1,128)S(1)}, f32[1,8192]{1,0:T(1,128)S(1)}, f32[1,8192]{1,0:T(1,128)S(1)}, f32[1,8192]{1,0:T(1,128)S(1)}, f32[1,8...) fusion(f32[1,8192]{1,0:T(1,128)S(1)} %get-tuple-element.130, ...), kind=kLoop, calls=%fused_computation.789 | loop fusion | flops 2220032 | bytes 3342336 | tf_op jit(solution)/shard_map/mul | solution.py:100
  391.3 17.4 %all_to_all.33 = f32[12,8,8,128]{3,2,1,0:T(8,128)S(1)} all-to-all(f32[12,8,8,128]{3,2,1,0:T(8,128)S(1)} %fusion.11), channel_id=1, replica_groups=mesh['gx'=8,'sp'=4] {'sp'}, dimensions={0} | all-to-all | bytes 786432 | tf_op jit(solution)/shard_map/all_to_all | solution.py:209
  (159 shorter events, 110.9 us)
Async XLA Ops:
  1.5 11.0 %collective-permute-start.1 = (f32[8,1,128]{2,1,0:T(1,128)S(1)}, f32[8,1,128]{2,1,0:T(1,128)S(1)}, u32[]{:S(2)}, u32[]{:S(2)}) collective-permute-start(f32[8,1,128]{2,1,0:T(1,128)S(1)} %get-tuple-element.281), channel_id=1, source_target_pairs={{4,0},{8,4},{12,8},{16,12},{20,16},{24,20},{28,24},{5,1},{9,5},{13... | collective-permute-start | bytes 12296 | tf_op jit(solution)/shard_map/ppermute | solution.py:24
  3.5 9.0 %collective-permute-start = (f32[8,1,128]{2,1,0:T(1,128)S(1)}, f32[8,1,128]{2,1,0:T(1,128)S(1)}, u32[]{:S(2)}, u32[]{:S(2)}) collective-permute-start(f32[8,1,128]{2,1,0:T(1,128)S(1)} %get-tuple-element.282), channel_id=1, source_target_pairs={{0,4},{4,8},{8,12},{12,16},{16,20},{20,24},{24,28},{1,5},{5,9},{9,... | collective-permute-start | bytes 12296 | tf_op jit(solution)/shard_map/ppermute | solution.py:22
  6.7 10.7 %collective-permute-start.4 = (f32[8,1,128]{2,1,0:T(1,128)S(1)}, f32[8,1,128]{2,1,0:T(1,128)S(1)}, u32[]{:S(2)}, u32[]{:S(2)}) collective-permute-start(f32[8,1,128]{2,1,0:T(1,128)S(1)} %get-tuple-element.283), channel_id=1, source_target_pairs={{0,4},{4,8},{8,12},{12,16},{16,20},{20,24},{24,28},{1,5},{5,9},{9,... | collective-permute-start | bytes 12296 | tf_op jit(solution)/shard_map/ppermute | solution.py:22
  10.5 6.9 %collective-permute-start.5 = (f32[8,1,128]{2,1,0:T(1,128)S(1)}, f32[8,1,128]{2,1,0:T(1,128)S(1)}, u32[]{:S(2)}, u32[]{:S(2)}) collective-permute-start(f32[8,1,128]{2,1,0:T(1,128)S(1)} %get-tuple-element.284), channel_id=1, source_target_pairs={{4,0},{8,4},{12,8},{16,12},{20,16},{24,20},{28,24},{5,1},{9,5},{13... | collective-permute-start | bytes 12296 | tf_op jit(solution)/shard_map/ppermute | solution.py:24
  12.6 11.4 %collective-permute-start.2 = (f32[8,10,1]{2,1,0:T(8,128)S(1)}, f32[8,10,1]{2,1,0:T(8,128)S(1)}, u32[]{:S(2)}, u32[]{:S(2)}) collective-permute-start(f32[8,10,1]{2,1,0:T(8,128)S(1)} %get-tuple-element.267), channel_id=1, source_target_pairs={{0,1},{1,2},{2,3},{4,5},{5,6},{6,7},{8,9},{9,10},{10,11},{12,13},{... | collective-permute-start | bytes 968 | tf_op jit(solution)/shard_map/ppermute | solution.py:22
  16.1 7.9 %collective-permute-start.3 = (f32[8,10,1]{2,1,0:T(8,128)S(1)}, f32[8,10,1]{2,1,0:T(8,128)S(1)}, u32[]{:S(2)}, u32[]{:S(2)}) collective-permute-start(f32[8,10,1]{2,1,0:T(8,128)S(1)} %get-tuple-element.268), channel_id=1, source_target_pairs={{1,0},{2,1},{3,2},{5,4},{6,5},{7,6},{9,8},{10,9},{11,10},{13,12},{... | collective-permute-start | bytes 968 | tf_op jit(solution)/shard_map/ppermute | solution.py:24
  17.5 6.8 %collective-permute-start.7 = (f32[8,10,1]{2,1,0:T(8,128)S(1)}, f32[8,10,1]{2,1,0:T(8,128)S(1)}, u32[]{:S(2)}, u32[]{:S(2)}) collective-permute-start(f32[8,10,1]{2,1,0:T(8,128)S(1)} %get-tuple-element.269), channel_id=1, source_target_pairs={{1,0},{2,1},{3,2},{5,4},{6,5},{7,6},{9,8},{10,9},{11,10},{13,12},{... | collective-permute-start | bytes 968 | tf_op jit(solution)/shard_map/ppermute | solution.py:24
  18.8 7.1 %collective-permute-start.6 = (f32[8,10,1]{2,1,0:T(8,128)S(1)}, f32[8,10,1]{2,1,0:T(8,128)S(1)}, u32[]{:S(2)}, u32[]{:S(2)}) collective-permute-start(f32[8,10,1]{2,1,0:T(8,128)S(1)} %get-tuple-element.270), channel_id=1, source_target_pairs={{0,1},{1,2},{2,3},{4,5},{5,6},{6,7},{8,9},{9,10},{10,11},{12,13},{... | collective-permute-start | bytes 968 | tf_op jit(solution)/shard_map/ppermute | solution.py:22
  53.3 5.6 %collective-permute-start.8 = (f32[8,1,128]{2,1,0:T(1,128)S(1)}, f32[8,1,128]{2,1,0:T(1,128)S(1)}, u32[]{:S(2)}, u32[]{:S(2)}) collective-permute-start(f32[8,1,128]{2,1,0:T(1,128)S(1)} %get-tuple-element.279), channel_id=1, source_target_pairs={{0,4},{4,8},{8,12},{12,16},{16,20},{20,24},{24,28},{1,5},{5,9},{9,... | collective-permute-start | bytes 12296 | tf_op jit(solution)/shard_map/ppermute | solution.py:22
  55.3 6.3 %collective-permute-start.9 = (f32[8,1,128]{2,1,0:T(1,128)S(1)}, f32[8,1,128]{2,1,0:T(1,128)S(1)}, u32[]{:S(2)}, u32[]{:S(2)}) collective-permute-start(f32[8,1,128]{2,1,0:T(1,128)S(1)} %get-tuple-element.280), channel_id=1, source_target_pairs={{4,0},{8,4},{12,8},{16,12},{20,16},{24,20},{28,24},{5,1},{9,5},{13... | collective-permute-start | bytes 12296 | tf_op jit(solution)/shard_map/ppermute | solution.py:24
  61.7 6.2 %collective-permute-start.11 = (f32[8,10,1]{2,1,0:T(8,128)S(1)}, f32[8,10,1]{2,1,0:T(8,128)S(1)}, u32[]{:S(2)}, u32[]{:S(2)}) collective-permute-start(f32[8,10,1]{2,1,0:T(8,128)S(1)} %get-tuple-element.265), channel_id=1, source_target_pairs={{1,0},{2,1},{3,2},{5,4},{6,5},{7,6},{9,8},{10,9},{11,10},{13,12},{... | collective-permute-start | bytes 968 | tf_op jit(solution)/shard_map/ppermute | solution.py:24
  63.0 6.4 %collective-permute-start.10 = (f32[8,10,1]{2,1,0:T(8,128)S(1)}, f32[8,10,1]{2,1,0:T(8,128)S(1)}, u32[]{:S(2)}, u32[]{:S(2)}) collective-permute-start(f32[8,10,1]{2,1,0:T(8,128)S(1)} %get-tuple-element.266), channel_id=1, source_target_pairs={{0,1},{1,2},{2,3},{4,5},{5,6},{6,7},{8,9},{9,10},{10,11},{12,13},{... | collective-permute-start | bytes 968 | tf_op jit(solution)/shard_map/ppermute | solution.py:22
  99.1 5.6 %collective-permute-start.12 = (f32[8,1,128]{2,1,0:T(1,128)S(1)}, f32[8,1,128]{2,1,0:T(1,128)S(1)}, u32[]{:S(2)}, u32[]{:S(2)}) collective-permute-start(f32[8,1,128]{2,1,0:T(1,128)S(1)} %get-tuple-element.277), channel_id=1, source_target_pairs={{0,4},{4,8},{8,12},{12,16},{16,20},{20,24},{24,28},{1,5},{5,9},{9,... | collective-permute-start | bytes 12296 | tf_op jit(solution)/shard_map/ppermute | solution.py:22
  101.0 6.7 %collective-permute-start.13 = (f32[8,1,128]{2,1,0:T(1,128)S(1)}, f32[8,1,128]{2,1,0:T(1,128)S(1)}, u32[]{:S(2)}, u32[]{:S(2)}) collective-permute-start(f32[8,1,128]{2,1,0:T(1,128)S(1)} %get-tuple-element.278), channel_id=1, source_target_pairs={{4,0},{8,4},{12,8},{16,12},{20,16},{24,20},{28,24},{5,1},{9,5},{13... | collective-permute-start | bytes 12296 | tf_op jit(solution)/shard_map/ppermute | solution.py:24
  107.7 134.0 %copy-start = (f32[3,8,8,512]{3,2,1,0:T(8,128)S(1)}, f32[3,8,8,512]{3,2,1,0:T(8,128)}, u32[]{:S(2)}) copy-start(f32[3,8,8,512]{3,2,1,0:T(8,128)} %param.15) | copy-start | bytes 1179652
  107.8 6.3 %collective-permute-start.15 = (f32[8,10,1]{2,1,0:T(8,128)S(1)}, f32[8,10,1]{2,1,0:T(8,128)S(1)}, u32[]{:S(2)}, u32[]{:S(2)}) collective-permute-start(f32[8,10,1]{2,1,0:T(8,128)S(1)} %get-tuple-element.263), channel_id=1, source_target_pairs={{1,0},{2,1},{3,2},{5,4},{6,5},{7,6},{9,8},{10,9},{11,10},{13,12},{... | collective-permute-start | bytes 968 | tf_op jit(solution)/shard_map/ppermute | solution.py:24
  109.2 6.4 %collective-permute-start.14 = (f32[8,10,1]{2,1,0:T(8,128)S(1)}, f32[8,10,1]{2,1,0:T(8,128)S(1)}, u32[]{:S(2)}, u32[]{:S(2)}) collective-permute-start(f32[8,10,1]{2,1,0:T(8,128)S(1)} %get-tuple-element.264), channel_id=1, source_target_pairs={{0,1},{1,2},{2,3},{4,5},{5,6},{6,7},{8,9},{9,10},{10,11},{12,13},{... | collective-permute-start | bytes 968 | tf_op jit(solution)/shard_map/ppermute | solution.py:22
  144.6 5.6 %collective-permute-start.16 = (f32[8,1,128]{2,1,0:T(1,128)S(1)}, f32[8,1,128]{2,1,0:T(1,128)S(1)}, u32[]{:S(2)}, u32[]{:S(2)}) collective-permute-start(f32[8,1,128]{2,1,0:T(1,128)S(1)} %get-tuple-element.275), channel_id=1, source_target_pairs={{0,4},{4,8},{8,12},{12,16},{16,20},{20,24},{24,28},{1,5},{5,9},{9,... | collective-permute-start | bytes 12296 | tf_op jit(solution)/shard_map/ppermute | solution.py:22
  146.5 6.7 %collective-permute-start.17 = (f32[8,1,128]{2,1,0:T(1,128)S(1)}, f32[8,1,128]{2,1,0:T(1,128)S(1)}, u32[]{:S(2)}, u32[]{:S(2)}) collective-permute-start(f32[8,1,128]{2,1,0:T(1,128)S(1)} %get-tuple-element.276), channel_id=1, source_target_pairs={{4,0},{8,4},{12,8},{16,12},{20,16},{24,20},{28,24},{5,1},{9,5},{13... | collective-permute-start | bytes 12296 | tf_op jit(solution)/shard_map/ppermute | solution.py:24
  153.3 6.2 %collective-permute-start.19 = (f32[8,10,1]{2,1,0:T(8,128)S(1)}, f32[8,10,1]{2,1,0:T(8,128)S(1)}, u32[]{:S(2)}, u32[]{:S(2)}) collective-permute-start(f32[8,10,1]{2,1,0:T(8,128)S(1)} %get-tuple-element.261), channel_id=1, source_target_pairs={{1,0},{2,1},{3,2},{5,4},{6,5},{7,6},{9,8},{10,9},{11,10},{13,12},{... | collective-permute-start | bytes 968 | tf_op jit(solution)/shard_map/ppermute | solution.py:24
  154.5 6.4 %collective-permute-start.18 = (f32[8,10,1]{2,1,0:T(8,128)S(1)}, f32[8,10,1]{2,1,0:T(8,128)S(1)}, u32[]{:S(2)}, u32[]{:S(2)}) collective-permute-start(f32[8,10,1]{2,1,0:T(8,128)S(1)} %get-tuple-element.262), channel_id=1, source_target_pairs={{0,1},{1,2},{2,3},{4,5},{5,6},{6,7},{8,9},{9,10},{10,11},{12,13},{... | collective-permute-start | bytes 968 | tf_op jit(solution)/shard_map/ppermute | solution.py:22
  190.1 5.6 %collective-permute-start.20 = (f32[8,1,128]{2,1,0:T(1,128)S(1)}, f32[8,1,128]{2,1,0:T(1,128)S(1)}, u32[]{:S(2)}, u32[]{:S(2)}) collective-permute-start(f32[8,1,128]{2,1,0:T(1,128)S(1)} %get-tuple-element.273), channel_id=1, source_target_pairs={{0,4},{4,8},{8,12},{12,16},{16,20},{20,24},{24,28},{1,5},{5,9},{9,... | collective-permute-start | bytes 12296 | tf_op jit(solution)/shard_map/ppermute | solution.py:22
  192.0 6.7 %collective-permute-start.21 = (f32[8,1,128]{2,1,0:T(1,128)S(1)}, f32[8,1,128]{2,1,0:T(1,128)S(1)}, u32[]{:S(2)}, u32[]{:S(2)}) collective-permute-start(f32[8,1,128]{2,1,0:T(1,128)S(1)} %get-tuple-element.274), channel_id=1, source_target_pairs={{4,0},{8,4},{12,8},{16,12},{20,16},{24,20},{28,24},{5,1},{9,5},{13... | collective-permute-start | bytes 12296 | tf_op jit(solution)/shard_map/ppermute | solution.py:24
  198.8 6.2 %collective-permute-start.23 = (f32[8,10,1]{2,1,0:T(8,128)S(1)}, f32[8,10,1]{2,1,0:T(8,128)S(1)}, u32[]{:S(2)}, u32[]{:S(2)}) collective-permute-start(f32[8,10,1]{2,1,0:T(8,128)S(1)} %get-tuple-element.259), channel_id=1, source_target_pairs={{1,0},{2,1},{3,2},{5,4},{6,5},{7,6},{9,8},{10,9},{11,10},{13,12},{... | collective-permute-start | bytes 968 | tf_op jit(solution)/shard_map/ppermute | solution.py:24
  200.1 6.4 %collective-permute-start.22 = (f32[8,10,1]{2,1,0:T(8,128)S(1)}, f32[8,10,1]{2,1,0:T(8,128)S(1)}, u32[]{:S(2)}, u32[]{:S(2)}) collective-permute-start(f32[8,10,1]{2,1,0:T(8,128)S(1)} %get-tuple-element.260), channel_id=1, source_target_pairs={{0,1},{1,2},{2,3},{4,5},{5,6},{6,7},{8,9},{9,10},{10,11},{12,13},{... | collective-permute-start | bytes 968 | tf_op jit(solution)/shard_map/ppermute | solution.py:22
  236.1 5.8 %collective-permute-start.24 = (f32[8,1,128]{2,1,0:T(1,128)S(1)}, f32[8,1,128]{2,1,0:T(1,128)S(1)}, u32[]{:S(2)}, u32[]{:S(2)}) collective-permute-start(f32[8,1,128]{2,1,0:T(1,128)S(1)} %get-tuple-element.271), channel_id=1, source_target_pairs={{0,4},{4,8},{8,12},{12,16},{16,20},{20,24},{24,28},{1,5},{5,9},{9,... | collective-permute-start | bytes 12296 | tf_op jit(solution)/shard_map/ppermute | solution.py:22
  238.0 6.7 %collective-permute-start.25 = (f32[8,1,128]{2,1,0:T(1,128)S(1)}, f32[8,1,128]{2,1,0:T(1,128)S(1)}, u32[]{:S(2)}, u32[]{:S(2)}) collective-permute-start(f32[8,1,128]{2,1,0:T(1,128)S(1)} %get-tuple-element.272), channel_id=1, source_target_pairs={{4,0},{8,4},{12,8},{16,12},{20,16},{24,20},{28,24},{5,1},{9,5},{13... | collective-permute-start | bytes 12296 | tf_op jit(solution)/shard_map/ppermute | solution.py:24
  244.8 19.5 %collective-permute-start.27 = (f32[8,10,1]{2,1,0:T(8,128)S(1)}, f32[8,10,1]{2,1,0:T(8,128)S(1)}, u32[]{:S(2)}, u32[]{:S(2)}) collective-permute-start(f32[8,10,1]{2,1,0:T(8,128)S(1)} %get-tuple-element.257), channel_id=1, source_target_pairs={{1,0},{2,1},{3,2},{5,4},{6,5},{7,6},{9,8},{10,9},{11,10},{13,12},{... | collective-permute-start | bytes 968 | tf_op jit(solution)/shard_map/ppermute | solution.py:24
  246.1 18.2 %collective-permute-start.26 = (f32[8,10,1]{2,1,0:T(8,128)S(1)}, f32[8,10,1]{2,1,0:T(8,128)S(1)}, u32[]{:S(2)}, u32[]{:S(2)}) collective-permute-start(f32[8,10,1]{2,1,0:T(8,128)S(1)} %get-tuple-element.258), channel_id=1, source_target_pairs={{0,1},{1,2},{2,3},{4,5},{5,6},{6,7},{8,9},{9,10},{10,11},{12,13},{... | collective-permute-start | bytes 968 | tf_op jit(solution)/shard_map/ppermute | solution.py:22
  303.7 5.8 %collective-permute-start.28 = (f32[5,8,1,512]{3,1,2,0:T(8,128)S(1)}, f32[5,8,1,512]{3,1,2,0:T(8,128)S(1)}, u32[]{:S(2)}, u32[]{:S(2)}) collective-permute-start(f32[5,8,1,512]{3,1,2,0:T(8,128)S(1)} %get-tuple-element.249), channel_id=1, source_target_pairs={{0,4},{4,8},{8,12},{12,16},{16,20},{20,24},{24,28},{1,5},{5,9},{9,... | collective-permute-start | bytes 245768 | tf_op jit(solution)/shard_map/ppermute | solution.py:22
  305.6 6.4 %collective-permute-start.29 = (f32[5,8,1,512]{3,1,2,0:T(8,128)S(1)}, f32[5,8,1,512]{3,1,2,0:T(8,128)S(1)}, u32[]{:S(2)}, u32[]{:S(2)}) collective-permute-start(f32[5,8,1,512]{3,1,2,0:T(8,128)S(1)} %get-tuple-element.250), channel_id=1, source_target_pairs={{4,0},{8,4},{12,8},{16,12},{20,16},{24,20},{28,24},{5,1},{9,5},{13... | collective-permute-start | bytes 245768 | tf_op jit(solution)/shard_map/ppermute | solution.py:24
  325.2 13.5 %all-to-all-start = ((f32[4,1,24576]{2,1,0:T(1,128)}), f32[4,1,24576]{2,1,0:T(1,128)S(1)}, u32[]{:S(2)}, u32[]{:S(2)}) async-start(f32[4,1,24576]{2,1,0:T(1,128)} %reshape.95), calls=%async_computation | async-start | bytes 786432 | tf_op jit(solution)/shard_map/all_to_all | solution.py:145
  (5 other events, 56.6 us)
